TPU v7x, 32 devices: a whole 2x2x4 slice. The times are simulated.
32 devices in a mesh: dp: 16 (over z, y, x), mp: 2 (over core).
Axes of the slice: x: 2, y: 2, z: 4, core: 2. Of those that a mesh axis runs over, the one named last changes fastest.
Arguments:
- tokens: bfloat16 [32768, 768], P('dp'), may hold values from -6 to 6
- segments: int32 [32768], P('dp'), may hold values from 0 to 31, as said below
- lengths: int32 [32, 32], P('dp'), may hold values from 0 to 1024, as said below
- ln1_gain: bfloat16 [768], replicated, may hold values from 0.25 to 1.75
- ln1_bias: bfloat16 [768], replicated, may hold values from -4 to 4
- w_qkv: bfloat16 [768, 3, 768], P(None, None, 'mp'), may hold values from -0.21875 to 0.21875
- b_qv: bfloat16 [2, 768], P(None, 'mp'), may hold values from -4 to 4
- w_out: bfloat16 [768, 768], P('mp'), may hold values from -0.625 to 0.625
- out_bias: bfloat16 [768], replicated, may hold values from -4 to 4
- ln2_gain: bfloat16 [768], replicated, may hold values from 0.25 to 1.75
- ln2_bias: bfloat16 [768], replicated, may hold values from -4 to 4
- w_fc: bfloat16 [768, 3072], P(None, 'mp'), may hold values from -0.21875 to 0.21875
- b_fc: bfloat16 [3072], P('mp'), may hold values from -4 to 4
- w_proj: bfloat16 [3072, 768], P('mp'), may hold values from -0.109375 to 0.109375
- proj_bias: bfloat16 [768], replicated, may hold values from -4 to 4
- cotangent: bfloat16 [32768, 768], P('dp'), may hold values from -17 to 17
Outputs:
- block_out: bfloat16 [32768, 768], P('dp')
- input_grad: float32 [32768, 768], P('dp')
- grad_ln1_gain: float32 [768], replicated
- grad_ln1_bias: float32 [768], replicated
- grad_w_qkv: float32 [768, 3, 768], P(None, None, 'mp')
- grad_b_qv: float32 [2, 768], P(None, 'mp')
- grad_w_out: float32 [768, 768], P('mp')
- grad_out_bias: float32 [768], replicated
- grad_ln2_gain: float32 [768], replicated
- grad_ln2_bias: float32 [768], replicated
- grad_w_fc: float32 [768, 3072], P(None, 'mp')
- grad_b_fc: float32 [3072], P('mp')
- grad_w_proj: float32 [3072, 768], P('mp')
- grad_proj_bias: float32 [768], replicated
Inputs may be any that keep to these rules, and one draw needn't show every extreme that they name: `segments`: within each bin of 1024 rows the document numbers start at 0, never fall and rise by one at each new document; a bin holds 1 to 32 documents; some bin holds 32. lengths[b, s] is the number of rows of bin b whose document number is s, 0 for numbers that the bin does not use; some bin is one document of 1024 rows.
All inputs are finite; a program needn't handle non-finite values.
Results may differ from a plain program's by a relative error of at most 0.009.
Values sent between devices are 32-bit elements; how exact they have to be, the bound alone decides.
A program may use at most 192 MiB of HBM per device.

v0:
```python
import jax
import jax.numpy as jnp
from jax import lax
from jax.sharding import PartitionSpec as P

HEAD_DIM = 64
BIN = 1024


epsilon = 1e-05
gelu_scale = 0.7978845608028654
gelu_cubic = 0.044715
score_scale = 0.125
masked_score = -1e30


def norm_parts(values):
    center = values - jnp.mean(values, axis=-1, keepdims=True)
    inverse = lax.rsqrt(jnp.mean(center * center, axis=-1, keepdims=True) + epsilon)
    return (center * inverse, inverse)


def norm_back(upstream, normal, inverse, gain):
    scaled = upstream * gain
    centered = scaled - jnp.mean(scaled, axis=-1, keepdims=True)
    return inverse * (centered - normal * jnp.mean(scaled * normal, axis=-1, keepdims=True))


def gelu_pair(values):
    inner_arg = gelu_scale * (values + gelu_cubic * values * values * values)
    tangent = jnp.tanh(inner_arg)
    output = 0.5 * values * (1.0 + tangent)
    derivative = 0.5 * (1.0 + tangent) + 0.5 * values * (1.0 - tangent * tangent) * gelu_scale * (
        1.0 + 3.0 * gelu_cubic * values * values
    )
    return (output, derivative)


def visible_pairs(seg_bin, start_bin):
    places = jnp.arange(seg_bin.shape[0], dtype=jnp.int32)
    causal = places[None, :] <= places[:, None]
    same_doc = seg_bin[None, :] == seg_bin[:, None]
    after_start = places[None, :] >= start_bin[:, None]
    return causal & same_doc & after_start


def masked_scores(queries, key_rows, seg_bin, start_bin):
    scores = (
        jnp.einsum("qhd,khd->hqk", queries, key_rows, preferred_element_type=jnp.float32)
        * score_scale
    )
    return jnp.where(visible_pairs(seg_bin, start_bin)[None], scores, masked_score)


def attend_forward(operands):
    joined_bin, seg_bin, start_bin = operands
    scores = masked_scores(joined_bin[:, 0], joined_bin[:, 1], seg_bin, start_bin)
    highest = jnp.max(scores, axis=-1, keepdims=True)
    weights = jnp.exp(scores - highest)
    totals = jnp.sum(weights, axis=-1, keepdims=True)
    attn_probs = (weights / totals).astype(jnp.bfloat16)
    mixed_rows = jnp.einsum(
        "hqk,khd->qhd", attn_probs, joined_bin[:, 2], preferred_element_type=jnp.float32
    )
    return (mixed_rows.astype(jnp.bfloat16), highest + jnp.log(totals))


def attend_backward(operands):
    joined_bin, seg_bin, start_bin, log_totals, upstream = operands
    queries = joined_bin[:, 0]
    key_rows = joined_bin[:, 1]
    value_rows = joined_bin[:, 2]
    attn_probs = jnp.exp(masked_scores(queries, key_rows, seg_bin, start_bin) - log_totals)
    dprobs = jnp.einsum("qhd,khd->hqk", upstream, value_rows, preferred_element_type=jnp.float32)
    inner_sum = jnp.sum(attn_probs * dprobs, axis=-1, keepdims=True)
    dscores = (attn_probs * (dprobs - inner_sum)).astype(jnp.bfloat16)
    grad_query = (
        jnp.einsum("hqk,khd->qhd", dscores, key_rows, preferred_element_type=jnp.float32)
        * score_scale
    )
    grad_key = (
        jnp.einsum("hqk,qhd->khd", dscores, queries, preferred_element_type=jnp.float32)
        * score_scale
    )
    grad_value = jnp.einsum(
        "hqk,qhd->khd",
        attn_probs.astype(jnp.bfloat16),
        upstream,
        preferred_element_type=jnp.float32,
    )
    return jnp.stack([grad_query, grad_key, grad_value], axis=1).astype(jnp.bfloat16)


def pack_flat(members, group_size):
    flat_vec = jnp.concatenate([member.reshape(-1) for member in members])
    padding = -flat_vec.shape[0] % group_size
    return jnp.concatenate([flat_vec, jnp.zeros((padding,), jnp.float32)])


def unpack_flat(flat_vec, members):
    result = []
    offset = 0
    for member in members:
        result.append(flat_vec[offset : offset + member.size].reshape(member.shape))
        offset = offset + member.size
    return result


def on_device(
    tokens,
    segments,
    lengths,
    ln1_gain,
    ln1_bias,
    w_qkv,
    b_qv,
    w_out,
    out_bias,
    ln2_gain,
    ln2_bias,
    w_fc,
    b_fc,
    w_proj,
    proj_bias,
    cotangent,
):
    gain_one = ln1_gain.astype(jnp.float32)
    bias_one = ln1_bias.astype(jnp.float32)
    qv_bias = b_qv.astype(jnp.float32)
    out_shift = out_bias.astype(jnp.float32)
    gain_two = ln2_gain.astype(jnp.float32)
    bias_two = ln2_bias.astype(jnp.float32)
    fc_shift = b_fc.astype(jnp.float32)
    proj_shift = proj_bias.astype(jnp.float32)
    token_rows = tokens.shape[0]
    bins_here = token_rows // BIN
    local_width = w_qkv.shape[2]
    local_heads = local_width // HEAD_DIM
    seg_bins = segments.reshape(bins_here, BIN)
    offsets = jnp.cumsum(lengths, axis=1) - lengths
    labels = jnp.arange(lengths.shape[1], dtype=jnp.int32)
    chosen = seg_bins[:, :, None] == labels[None, None, :]
    start_bins = jnp.sum(jnp.where(chosen, offsets[:, None, :], 0), axis=2)
    inputs_f = tokens.astype(jnp.float32)
    normal_one, inverse_one = norm_parts(inputs_f)
    normed_one = (normal_one * gain_one + bias_one).astype(jnp.bfloat16)
    bias_rows = jnp.stack([qv_bias[0], jnp.zeros_like(qv_bias[0]), qv_bias[1]])
    joined_qkv = jnp.einsum("td,dcj->tcj", normed_one, w_qkv, preferred_element_type=jnp.float32)
    joined_qkv = (joined_qkv + bias_rows[None]).astype(jnp.bfloat16)
    joined_bins = joined_qkv.reshape(bins_here, BIN, 3, local_heads, HEAD_DIM)
    mixed_bins, log_totals = lax.map(attend_forward, (joined_bins, seg_bins, start_bins))
    mixed_rows = mixed_bins.reshape(token_rows, local_width)
    attn_part = jnp.dot(mixed_rows, w_out, preferred_element_type=jnp.float32)
    first_sum = inputs_f + lax.psum(attn_part, "mp") + out_shift
    normal_two, inverse_two = norm_parts(first_sum)
    normed_two = (normal_two * gain_two + bias_two).astype(jnp.bfloat16)
    hidden_pre = jnp.dot(normed_two, w_fc, preferred_element_type=jnp.float32) + fc_shift
    hidden_act, hidden_slope = gelu_pair(hidden_pre)
    hidden_low = hidden_act.astype(jnp.bfloat16)
    proj_part = jnp.dot(hidden_low, w_proj, preferred_element_type=jnp.float32)
    block_sum = first_sum + lax.psum(proj_part, "mp") + proj_shift
    block_out = block_sum.astype(jnp.bfloat16)
    upstream = cotangent.astype(jnp.float32)
    grad_proj_weight = jnp.einsum(
        "tf,td->fd", hidden_low, cotangent, preferred_element_type=jnp.float32
    )
    grad_proj_shift = jnp.sum(upstream, axis=0)
    grad_hidden = jnp.einsum("td,fd->tf", cotangent, w_proj, preferred_element_type=jnp.float32)
    grad_pre = (grad_hidden * hidden_slope).astype(jnp.bfloat16)
    grad_fc_weight = jnp.einsum(
        "td,tf->df", normed_two, grad_pre, preferred_element_type=jnp.float32
    )
    grad_fc_shift = jnp.sum(grad_pre.astype(jnp.float32), axis=0)
    normed_two_part = jnp.einsum("tf,df->td", grad_pre, w_fc, preferred_element_type=jnp.float32)
    grad_normed_two = lax.psum(normed_two_part, "mp")
    grad_gain_two = jnp.sum(grad_normed_two * normal_two, axis=0)
    grad_bias_two = jnp.sum(grad_normed_two, axis=0)
    grad_first = upstream + norm_back(grad_normed_two, normal_two, inverse_two, gain_two)
    mlp_terms = [
        grad_fc_weight,
        grad_fc_shift,
        grad_proj_weight,
        grad_proj_shift,
        grad_gain_two,
        grad_bias_two,
    ]
    group_count = lax.axis_size("dp")
    grad_branch = grad_first.astype(jnp.bfloat16)
    grad_out_weight = jnp.einsum(
        "tj,td->jd", mixed_rows, grad_branch, preferred_element_type=jnp.float32
    )
    grad_out_shift = jnp.sum(grad_branch.astype(jnp.float32), axis=0)
    grad_mixed = jnp.einsum(
        "td,jd->tj", grad_branch, w_out, preferred_element_type=jnp.float32
    ).astype(jnp.bfloat16)
    grad_mixed_bins = grad_mixed.reshape(bins_here, BIN, local_heads, HEAD_DIM)
    grad_joined_bins = lax.map(
        attend_backward, (joined_bins, seg_bins, start_bins, log_totals, grad_mixed_bins)
    )
    grad_joined = grad_joined_bins.reshape(token_rows, 3, local_width)
    grad_qkv_weight = jnp.einsum(
        "td,tcj->dcj", normed_one, grad_joined, preferred_element_type=jnp.float32
    )
    joined_totals = jnp.sum(grad_joined.astype(jnp.float32), axis=0)
    grad_qv_bias = jnp.stack([joined_totals[0], joined_totals[2]])
    normed_one_part = jnp.einsum(
        "tcj,dcj->td", grad_joined, w_qkv, preferred_element_type=jnp.float32
    )
    grad_normed_one = lax.psum(normed_one_part, "mp")
    grad_gain_one = jnp.sum(grad_normed_one * normal_one, axis=0)
    grad_bias_one = jnp.sum(grad_normed_one, axis=0)
    input_grad = grad_first + norm_back(grad_normed_one, normal_one, inverse_one, gain_one)
    attn_terms = [
        grad_qkv_weight,
        grad_qv_bias,
        grad_out_weight,
        grad_out_shift,
        grad_gain_one,
        grad_bias_one,
    ]
    both_terms = attn_terms + mlp_terms
    both_shards = lax.psum_scatter(
        pack_flat(both_terms, group_count), "dp", scatter_dimension=0, tiled=True
    )
    both_sums = unpack_flat(lax.all_gather(both_shards, "dp", axis=0, tiled=True), both_terms)
    attn_sums = both_sums[: len(attn_terms)]
    mlp_sums = both_sums[len(attn_terms) :]
    return (
        block_out,
        input_grad,
        attn_sums[4],
        attn_sums[5],
        attn_sums[0],
        attn_sums[1],
        attn_sums[2],
        attn_sums[3],
        mlp_sums[4],
        mlp_sums[5],
        mlp_sums[0],
        mlp_sums[1],
        mlp_sums[2],
        mlp_sums[3],
    )


def solution(mesh):
    placed = (
        P("dp", None),
        P("dp"),
        P("dp", None),
        P(),
        P(),
        P(None, None, "mp"),
        P(None, "mp"),
        P("mp", None),
        P(),
        P(),
        P(),
        P(None, "mp"),
        P("mp"),
        P("mp", None),
        P(),
        P("dp", None),
    )
    return jax.shard_map(
        on_device,
        mesh=mesh,
        in_specs=placed,
        out_specs=(
            P("dp", None),
            P("dp", None),
            P(),
            P(),
            P(None, None, "mp"),
            P(None, "mp"),
            P("mp", None),
            P(),
            P(),
            P(),
            P(None, "mp"),
            P("mp"),
            P("mp", None),
            P(),
        ),
        check_vma=False,
    )
```

profile of v0, /device:TPU:0, one launch (start us, length us, event | category | flops | bytes accessed | tf_op | source)
XLA Modules:
  0.0 1430.0 jit_solution(74209950715607548)
XLA Ops:
  13.6 6.5 add_convert_fusion
  20.1 6.6 copy.74
  26.7 8.8 reshape.354
  35.6 6.1 copy.75
  42.0 75.4 %while.22 = (s32[]{:T(128)}, bf16[2,1024,6,64]{1,3,2,0:T(8,128)(2,1)}, f32[2,6,1024,1]{2,1,3,0:T(8,128)}, bf16[2,1024,3,6,64]{1,4,3,2,0:T(8,128)(2,1)}, s32[2,10...) while((s32[]{:T(128)}, bf16[2,1024,6,64]{1,3,2,0:T(8,128)(2,1)}, f32[2,6,1024,1]{2,1,3,0:T(8,128)}, ...), condition=%wide.region_7.8_spmd, body=%wide.region_4.7_spmd.sunk | while | flops 1691740160 | bytes 87802960 | solution.py:151
  44.7 10.6 fusion.111
  55.3 11.2 fusion.112
  67.2 12.4 fusion.113
  82.3 10.6 fusion.111
  92.9 11.2 fusion.112
  104.8 12.4 fusion.113
  126.9 34.9 %all-reduce.9.cloned.1.call-done = f32[2048,768]{1,0:T(8,128)} async-done(((f32[2048,768]{1,0:T(8,128)}), f32[2048,768]{1,0:T(8,128)}) %all-reduce.9.cloned.1.call-update) | async-done | bytes 6291472 | tf_op jit(solution)/shard_map/psum | solution.py:154
  167.4 11.0 multiply_convert_fusion.3
  178.4 14.0 convert_reduce_fusion
  195.0 6.9 fusion.75
  202.0 10.3 all-reduce.17.cloned.1.call-start
  212.2 14.2 fusion.64
  226.4 6.0 reshape.362
  232.5 10.1 fusion.76
  248.4 9.6 fusion.74
  258.1 6.6 multiply_reduce_fusion.1
  283.9 153.9 %while.23 = (s32[]{:T(128)}, bf16[2,1024,3,6,64]{1,4,3,2,0:T(8,128)(2,1)}, bf16[2,1024,3,6,64]{1,4,3,2,0:T(8,128)(2,1)}, s32[2,1024]{1,0:T(2,128)S(1)}, s32[2,10...) while((s32[]{:T(128)}, ...), condition=%wide.region_17.18_spmd, body=%wide.region_15.17_spmd.sunk | while | flops 4135184384 | bytes 267076784 | solution.py:197
  287.1 10.1 fusion.118
  298.0 17.1 %multiply_reduce_fusion.7 = (f32[6,1024]{1,0:T(8,128)S(1)}, f32[6,1024,1024]{1,2,0:T(8,128)}) fusion(f32[6,1024,1024]{1,2,0:T(8,128)} %fusion.118, f32[6,1024]{1,0:T(8,128)S(1)} %dynamic-slice_bitcast_fusion.8, pred[1024,1024]{0,1:T(8,128)(4,1)S(1)} %fusion.119, bf16[1024,3,6,64]{0,3,2,1:T(8,128)(2,1)S(1)} %dynamic-slice_bitcast_fusion.7, ...), kind=kOutput, calls=%fused_computation.24.clone.1 | convolution fusion | flops 836757504 | bytes 53010944 | tf_op jit(solution)/shard_map/while/body/eval_jaxpr/qhd,khd->hqk/dot_general | solution.py:74
  315.0 17.2 %multiply_convert_fusion.5 = bf16[6,1024,1024]{1,2,0:T(8,128)(2,1)S(1)} fusion(f32[6,1024,1024]{1,2,0:T(8,128)} %get-tuple-element.345, f32[6,1024,1024]{1,2,0:T(8,128)} %fusion.118, f32[6,1024]{1,0:T(8,128)S(1)} %get-tuple-element.346, f32[6,1024]{1,0:T(8,128)S(1)} %dynamic-slice_bitcast_fusion.8, pred[1024,1024]{0,1:T(8,128)(4,1)S(1)} %fusion.119), kind=kLoop, calls=%fused_computation.23.clone.1 | loop fusion | flops 37748736 | bytes 64012288 | tf_op jit(solution)/shard_map/while/body/eval_jaxpr/convert_element_type | solution.py:76
  339.2 8.6 fusion.121
  347.8 11.6 fusion.120
  363.8 10.1 fusion.118
  374.6 17.1 %multiply_reduce_fusion.7 = (f32[6,1024]{1,0:T(8,128)S(1)}, f32[6,1024,1024]{1,2,0:T(8,128)}) fusion(f32[6,1024,1024]{1,2,0:T(8,128)} %fusion.118, f32[6,1024]{1,0:T(8,128)S(1)} %dynamic-slice_bitcast_fusion.8, pred[1024,1024]{0,1:T(8,128)(4,1)S(1)} %fusion.119, bf16[1024,3,6,64]{0,3,2,1:T(8,128)(2,1)S(1)} %dynamic-slice_bitcast_fusion.7, ...), kind=kOutput, calls=%fused_computation.24.clone.1 | convolution fusion | flops 836757504 | bytes 53010944 | tf_op jit(solution)/shard_map/while/body/eval_jaxpr/qhd,khd->hqk/dot_general | solution.py:74
  391.7 17.2 %multiply_convert_fusion.5 = bf16[6,1024,1024]{1,2,0:T(8,128)(2,1)S(1)} fusion(f32[6,1024,1024]{1,2,0:T(8,128)} %get-tuple-element.345, f32[6,1024,1024]{1,2,0:T(8,128)} %fusion.118, f32[6,1024]{1,0:T(8,128)S(1)} %get-tuple-element.346, f32[6,1024]{1,0:T(8,128)S(1)} %dynamic-slice_bitcast_fusion.8, pred[1024,1024]{0,1:T(8,128)(4,1)S(1)} %fusion.119), kind=kLoop, calls=%fused_computation.23.clone.1 | loop fusion | flops 37748736 | bytes 64012288 | tf_op jit(solution)/shard_map/while/body/eval_jaxpr/convert_element_type | solution.py:76
  415.8 8.6 fusion.121
  424.4 11.6 fusion.120
  441.0 9.4 copy.80
  454.6 8.8 reshape.358
  463.5 10.3 fusion.58
  473.7 6.5 convolution_bitcast_fusion
  480.5 6.6 copy.84
  487.1 7.0 reshape.359
  500.9 10.9 dynamic-update-slice.3
  513.1 15.6 %all-reduce.17.cloned.1.call-done = (f32[2048,768]{1,0:T(8,128)}, f32[2048,768]{1,0:T(8,128)}) async-done(((f32[2048,768]{1,0:T(8,128)}, f32[2048,768]{1,0:T(8,128)}), (f32[2048,768]{1,0:T(8,128)}, f32[2048,768]{1,0:T(8,128)})) %all-reduce.17.cloned.1.call-update) | async-done | bytes 12582928 | tf_op jit(solution)/shard_map/psum | solution.py:161
  540.4 40.9 %dynamic-update-slice.9 = f32[3545856]{0:T(1024)} dynamic-update-slice(f32[3545856]{0:T(1024)} %constant_dynamic-update-slice_fusion.3, f32[1179648]{0:T(1024)} %reshape.363, s32[]{} %constant.97) | dynamic-update-slice | bytes 9437188
  587.0 394.1 %all-reduce.15.cloned.1.call-done = f32[3545856]{0:T(1024)} async-done(((f32[3545856]{0:T(1024)}), f32[3545856]{0:T(1024)}) %all-reduce.15.cloned.1.call-update) | async-done | bytes 14183440
  990.5 8.3 add_convert_fusion.1
  998.8 7.4 fusion.53
  1006.2 378.0 %all-reduce.13.cloned.1.call-done = f32[3545856]{0:T(1024)} async-done(((f32[3545856]{0:T(1024)}), f32[3545856]{0:T(1024)}) %all-reduce.13.cloned.1.call-update) | async-done | bytes 14183440
  1384.2 6.4 fusion.69
  1396.3 6.0 slice.132
  1406.3 6.4 slice.121
  (194 shorter events, 141.1 us)
Async XLA Ops:
  7.2 160.2 %copy-start = (bf16[768,1536]{1,0:T(8,128)(2,1)S(1)}, bf16[768,1536]{1,0:T(8,128)(2,1)}, u32[]{:S(2)}) copy-start(bf16[768,1536]{1,0:T(8,128)(2,1)} %param.31) | copy-start | bytes 7077892
  7.2 5.8 copy-start.32
  7.2 5.8 copy-start.27
  7.2 5.8 copy-start.33
  7.2 154.6 %all-reduce.9.cloned.1.call-start = ((), (), s32[]{:S(2)}) async-start(), calls=%async_computation | async-start | bytes 12582912 | tf_op jit(solution)/shard_map/psum | solution.py:154
  7.3 6.3 copy-start.5
  7.3 6.3 copy-start.41
  9.9 3.4 copy-start.15
  35.5 6.1 copy-start.25
  35.5 6.1 copy-start.29
  117.4 4.7 copy-start.14
  121.0 1.2 copy-start.9
  122.2 4.6 copy-start.34
  122.2 4.7 copy-start.35
  122.2 4.7 copy-start.28
  122.2 4.7 copy-start.36
  126.8 131.3 %all-reduce.11.cloned.1.call-start = ((), (), s32[]{:S(2)}) async-start(), calls=%async_computation.1 | async-start | bytes 12582912 | tf_op jit(solution)/shard_map/psum | solution.py:175
  166.4 12.0 copy-start.3
  167.3 11.1 copy-start.12
  167.4 11.1 copy-start.39
  192.4 2.6 copy-start.43
  202.0 326.8 %all-reduce.17.cloned.1.call-start = ((), (), s32[]{:S(2)}) async-start(), calls=%async_computation.4 | async-start | bytes 25165824 | tf_op jit(solution)/shard_map/psum | solution.py:161
  242.6 5.9 copy-start.40
  258.1 6.6 copy-start.7
  258.1 7.4 copy-start.13
  271.2 2.6 copy-start.4
  332.2 4.6 copy-start.2
  339.2 8.6 copy-start.8
  408.9 4.6 copy-start.2
  415.8 8.6 copy-start.8
  437.8 12.6 copy-start.10
  454.6 8.9 copy-start.16
  454.6 8.8 copy-start.18
  454.6 8.8 copy-start.20
  454.6 8.8 copy-start.31
  463.4 10.3 copy-start.11
  463.5 10.3 copy-start.42
  480.2 500.9 %all-reduce.15.cloned.1.call-start = ((), (), s32[]{:S(2)}) async-start(), calls=%async_computation.3 | async-start | bytes 28368896
  494.1 17.8 %copy-start.24 = (f32[768]{0:T(1024)S(1)}, f32[768]{0:T(1024)}, u32[]{:S(2)}) copy-start(f32[768]{0:T(1024)} %get-tuple-element.217) | copy-start | bytes 9220
  499.6 37.1 %slice-start = ((s8[4718592]{0:T(1024)(128)(4,1)}), s8[524288]{0:T(1024)(128)(4,1)S(1)}, s32[]{:S(2)}) async-start(s8[4718592]{0:T(1024)(128)(4,1)} %bitcast.152), calls=%async_computation.5 | async-start | bytes 1048576
  528.8 7.9 slice-start.1
  534.1 5.0 copy-start.26
  539.0 42.3 %copy-start.23 = (f32[768]{0:T(1024)S(1)}, f32[768]{0:T(1024)}, u32[]{:S(2)}) copy-start(f32[768]{0:T(1024)} %get-tuple-element.238) | copy-start | bytes 9220
  539.0 43.6 %copy-start.22 = (f32[768]{0:T(1024)S(1)}, f32[768]{0:T(1024)}, u32[]{:S(2)}) copy-start(f32[768]{0:T(1024)} %get-tuple-element.181) | copy-start | bytes 9220
  539.0 44.9 %copy-start.21 = (f32[768]{0:T(1024)S(1)}, f32[768]{0:T(1024)}, u32[]{:S(2)}) copy-start(f32[768]{0:T(1024)} %get-tuple-element.187) | copy-start | bytes 9220
  584.5 799.7 %all-reduce.13.cloned.1.call-start = ((), (), s32[]{:S(2)}) async-start(), calls=%async_computation.2 | async-start | bytes 28368896
  990.5 8.3 copy-start.6
  1406.3 16.7 %copy-start.1 = (bf16[768,1536]{1,0:T(8,128)(2,1)S(1)}, bf16[768,1536]{1,0:T(8,128)(2,1)}, u32[]{:S(2)}) copy-start(bf16[768,1536]{1,0:T(8,128)(2,1)} %param.31) | copy-start | bytes 7077892
  (5 other events, 3.1 us)
Sparse Core Ops, SparseCore 0:
  126.9 34.9 all-reduce.8
  202.1 33.3 all-reduce.10
  480.4 48.3 all-reduce.16
  584.6 396.4 all-reduce.14
  989.9 394.1 all-reduce.12
where the time goes:
time: 1440 us; the launch traced here: 1430 us
  waiting for transfers between devices  823 us (57%)
  matrix products  246 us (17%)
  local copies, waits for them, and re-layouts  221 us (15%)
  other arithmetic  113 us (8%)
  between operations  16.1 us (1%)
    unnamed x7, waiting for transfers between devices  772 us
    unnamed x104, local copies, waits for them, and re-layouts  91.7 us
    dot_general x4, matrix products, masked_scores(): jnp.einsum('qhd,khd->hqk', queries, key_rows, preferred_element_type=jnp....  41.4 us
    psum x1, waiting for transfers between devices, on_device(): first_sum = inputs_f + lax.psum(attn_part, 'mp') + out_shift  34.9 us
    convert_element_type x2, other arithmetic, attend_backward(): dscores = (attn_probs * (dprobs - inner_sum)).astype(jnp.bfloat16)  34.3 us
    dot_general x2, matrix products, attend_backward(): jnp.einsum('qhd,khd->hqk', upstream, value_rows, preferred_element_type=j...  34.1 us
  transfers between devices with their start and end apart: 5, of which 4 were waited for; matrix products, arithmetic and copies ran while one was open for 7% of the time, Pallas kernels for 0%

commit v1 on v0

v1 whole, which is shorter than its diff:
```python
import functools

import jax
import jax.numpy as jnp
from jax import lax
from jax.experimental import pallas as pl
from jax.experimental.pallas import tpu as pltpu
from jax.sharding import PartitionSpec as P

HEAD_DIM = 64
BIN = 1024
PAIR = 2 * HEAD_DIM
BLOCK = 256
CHUNK = 256
SLOTS = 6
AHEAD = 2
DELAY = 2

epsilon = 1e-05
gelu_scale = 0.7978845608028654
gelu_cubic = 0.044715
score_scale = 0.125
masked_score = -1e30

MESH = pl.DeviceIdType.MESH
F32 = jnp.float32
BF16 = jnp.bfloat16
VMEM_LIMIT = 64_000_000


def dot_nn(left, right):
    return lax.dot_general(left, right, (((1,), (0,)), ((), ())), preferred_element_type=F32)


def dot_nt(left, right):
    return lax.dot_general(left, right, (((1,), (1,)), ((), ())), preferred_element_type=F32)


def dot_tn(left, right):
    return lax.dot_general(left, right, (((0,), (0,)), ((), ())), preferred_element_type=F32)


def norm_parts(values):
    center = values - jnp.mean(values, axis=-1, keepdims=True)
    inverse = lax.rsqrt(jnp.mean(center * center, axis=-1, keepdims=True) + epsilon)
    return center * inverse, inverse


def norm_back(upstream, normal, inverse, gain):
    scaled = upstream * gain
    centered = scaled - jnp.mean(scaled, axis=-1, keepdims=True)
    return inverse * (centered - normal * jnp.mean(scaled * normal, axis=-1, keepdims=True))


def gelu_pair(values):
    square = values * values
    tangent = jnp.tanh(gelu_scale * (values + gelu_cubic * square * values))
    half = 0.5 * (1.0 + tangent)
    slope = half + 0.5 * values * (1.0 - tangent * tangent) * (
        gelu_scale + 3.0 * gelu_cubic * gelu_scale * square
    )
    return values * half, slope


def column_to_row(column):
    rows = column.shape[0]
    return jnp.broadcast_to(column, (rows, 128)).T[0:1]


def head_mask(head, scale):
    lane = lax.broadcasted_iota(jnp.int32, (1, PAIR), 1)
    return jnp.where(lane // HEAD_DIM == head, scale, 0.0).astype(BF16)


def attend_pair(qkv_ref, start_ref, attn_ref, lse_ref):
    lane = lax.broadcasted_iota(jnp.int32, (1, PAIR), 1)
    for block in range(BIN // BLOCK):
        rows = slice(block * BLOCK, (block + 1) * BLOCK)
        seen = (block + 1) * BLOCK
        queries = qkv_ref[0, 0, rows]
        key_rows = qkv_ref[0, 1, 0:seen]
        value_rows = qkv_ref[0, 2, 0:seen]
        j = lax.broadcasted_iota(jnp.int32, (BLOCK, seen), 1)
        i = lax.broadcasted_iota(jnp.int32, (BLOCK, seen), 0) + block * BLOCK
        visible = (j >= start_ref[rows]) & (j <= i)
        mixed = []
        for head in range(2):
            scores = dot_nt(queries * head_mask(head, score_scale), key_rows)
            scores = jnp.where(visible, scores, masked_score)
            highest = jnp.max(scores, axis=-1, keepdims=True)
            weights = jnp.exp(scores - highest)
            totals = jnp.sum(weights, axis=-1, keepdims=True)
            mixed.append(dot_nn(weights.astype(BF16), value_rows) / totals)
            lse_ref[0, head : head + 1, rows] = column_to_row(highest + jnp.log(totals))
        attn_ref[0, rows] = jnp.where(lane < HEAD_DIM, mixed[0], mixed[1]).astype(BF16)


def project_and_attend(h1, w_ref, bias_ref, start_ref, qkv_ref, attn_ref, lse_ref):
    for c in range(3):
        out = dot_nn(h1, w_ref[c].astype(BF16)) + bias_ref[c : c + 1]
        qkv_ref[0, c] = out.astype(BF16)
    attend_pair(qkv_ref, start_ref, attn_ref, lse_ref)


def own_front_kernel(
    mp_ref, x_ref, seg_ref, len_ref, gain_ref, shift_ref, w_ref, bias_ref,
    qkv_ref, attn_ref, lse_ref, h1_ref, start_ref, row_ref,
):
    @pl.when(pl.program_id(0) == 0)
    def _():
        gain = gain_ref[...].astype(F32)
        shift = shift_ref[...].astype(F32)
        for block in range(BIN // BLOCK):
            rows = slice(block * BLOCK, (block + 1) * BLOCK)
            normal, _ = norm_parts(x_ref[rows].astype(F32))
            h1_ref[rows] = (normal * gain + shift).astype(BF16)
        mine = mp_ref[0]
        count = len_ref.shape[1]
        seg = seg_ref[pl.ds(mine, 1), :].astype(F32)
        seg = jnp.broadcast_to(seg, (128, BIN)).T
        seg = seg[:, :count]
        label = lax.broadcasted_iota(jnp.int32, (BIN, count), 1).astype(F32)
        sizes = len_ref[pl.ds(mine, 1), :].astype(F32)
        start = jnp.sum(jnp.where(label < seg, sizes, 0.0), axis=1, keepdims=True)
        rows_of = jnp.sum(jnp.where(label == seg, 1.0, 0.0), axis=0, keepdims=True)
        first = jnp.sum(jnp.where(label < seg, rows_of, 0.0), axis=1, keepdims=True)
        start = jnp.maximum(start, first)
        start_ref[...] = start.astype(jnp.int32)
        row_ref[...] = column_to_row(start).astype(jnp.int32)

    project_and_attend(h1_ref[...], w_ref, bias_ref, start_ref, qkv_ref, attn_ref, lse_ref)


def other_front_kernel(h1_ref, start_ref, w_ref, bias_ref, qkv_ref, attn_ref, lse_ref):
    project_and_attend(h1_ref[...], w_ref, bias_ref, start_ref, qkv_ref, attn_ref, lse_ref)


def fixed(shape):
    return pl.BlockSpec(shape, lambda *_: (0,) * len(shape), pipeline_mode=pl.Buffered(1))


def front(mine, x, seg, lens, gain, shift, w_own, bias_own, width):
    model = x.shape[1]
    pairs = width // PAIR
    per_pair = [
        pl.BlockSpec((3, model, PAIR), lambda p, *_: (0, 0, p)),
        pl.BlockSpec((3, PAIR), lambda p, *_: (0, p)),
    ]
    outs = [
        pl.BlockSpec((1, 3, BIN, PAIR), lambda p, *_: (p, 0, 0, 0)),
        pl.BlockSpec((1, BIN, PAIR), lambda p, *_: (p, 0, 0)),
        pl.BlockSpec((1, 8, BIN), lambda p, *_: (p, 0, 0)),
    ]
    out_shapes = [
        jax.ShapeDtypeStruct((pairs, 3, BIN, PAIR), BF16),
        jax.ShapeDtypeStruct((pairs, BIN, PAIR), BF16),
        jax.ShapeDtypeStruct((pairs, 8, BIN), F32),
    ]
    cost = pl.CostEstimate(flops=6_000_000_000, bytes_accessed=10_000_000, transcendentals=0)
    params = pltpu.CompilerParams(vmem_limit_bytes=VMEM_LIMIT)
    own = pl.pallas_call(
        own_front_kernel,
        out_shape=out_shapes
        + [
            jax.ShapeDtypeStruct((BIN, model), BF16),
            jax.ShapeDtypeStruct((BIN, 1), jnp.int32),
            jax.ShapeDtypeStruct((1, BIN), jnp.int32),
        ],
        grid_spec=pltpu.PrefetchScalarGridSpec(
            num_scalar_prefetch=1,
            grid=(pairs,),
            in_specs=[
                pl.BlockSpec((BIN, model), lambda p, m: (m[0], 0)),
                fixed(seg.shape), fixed(lens.shape), fixed((1, model)), fixed((1, model)),
            ]
            + per_pair,
            out_specs=outs
            + [
                pl.BlockSpec((BIN, model), lambda p, *_: (0, 0)),
                pl.BlockSpec((BIN, 1), lambda p, *_: (0, 0)),
                pl.BlockSpec((1, BIN), lambda p, *_: (0, 0)),
            ],
        ),
        compiler_params=params,
        cost_estimate=cost,
        name="own_front",
    )

    def other(h1, start, w_other, bias_other):
        return pl.pallas_call(
            other_front_kernel,
            out_shape=out_shapes,
            grid=(pairs,),
            in_specs=[fixed((BIN, model)), fixed((BIN, 1))] + per_pair,
            out_specs=outs,
            compiler_params=params,
            cost_estimate=cost,
            name="other_front",
        )(h1, start, w_other, bias_other)

    return own(mine, x, seg, lens, gain, shift, w_own, bias_own), other


def middle_kernel(
    mp_ref, x_ref, cot_ref, attn_own_ref, attn_other_ref, vec_in_ref, bfc_ref,
    wo_own_ref, wo_f_ref, wf_own_ref, wf_f_ref, wp_own_ref, wp_f_ref,
    g_ref, df_ref, h2_ref, da_ref, dattn_ref, dr1_ref, sum_ref, vec_ref,
    wo_other_ref, wf_other_ref, wp_other_ref,
):
    @pl.when(pl.program_id(0) == 0)
    def _():
        wo_other_ref[...] = wo_f_ref[...].astype(BF16)
        wf_other_ref[...] = wf_f_ref[...].astype(BF16)
        wp_other_ref[...] = wp_f_ref[...].astype(BF16)
        vec_ref[...] = jnp.zeros_like(vec_ref)

    pairs = attn_own_ref.shape[0]
    model = x_ref.shape[1]
    hidden = wf_own_ref.shape[1]
    out_bias = vec_in_ref[0:1]
    gain = vec_in_ref[1:2]
    shift = vec_in_ref[2:3]
    x = x_ref[...].astype(F32)
    cot = cot_ref[...]
    upstream = cot.astype(F32)
    mixed_own = jnp.concatenate([attn_own_ref[p] for p in range(pairs)], axis=1)
    mixed_other = jnp.concatenate([attn_other_ref[p] for p in range(pairs)], axis=1)
    branch = dot_nn(mixed_own, wo_own_ref[...]) + dot_nn(mixed_other, wo_other_ref[...])
    first = x + (branch + out_bias)
    normal, inverse = norm_parts(first)
    h2 = (normal * gain + shift).astype(BF16)
    h2_ref[...] = h2
    total = first
    dh2 = jnp.zeros_like(first)
    for half in range(2):
        wf = (wf_own_ref, wf_other_ref)[half]
        wp = (wp_own_ref, wp_other_ref)[half]
        pre = dot_nn(h2, wf[...]) + bfc_ref[half : half + 1]
        act, slope = gelu_pair(pre)
        act = act.astype(BF16)
        g_ref[half] = act
        total = total + dot_nn(act, wp[...])
        df = (dot_nt(cot, wp[...]) * slope).astype(BF16)
        df_ref[half] = df
        dh2 = dh2 + dot_nt(df, wf[...])
        df_sum = jnp.sum(df.astype(F32), axis=0, keepdims=True)
        for piece in range(hidden // model):
            cols = slice(piece * model, (piece + 1) * model)
            row = slice(6 + piece, 7 + piece)
            vec_ref[half, row] = vec_ref[half, row] + df_sum[:, cols]
    sum_ref[...] = total
    dr1 = upstream + norm_back(dh2, normal, inverse, gain)
    dr1_ref[...] = dr1
    da = dr1.astype(BF16)
    da_ref[...] = da
    for half in range(2):
        wo = (wo_own_ref, wo_other_ref)[half]
        dattn = dot_nt(da, wo[...]).astype(BF16)
        for p in range(pairs):
            dattn_ref[half * pairs + p] = dattn[:, p * PAIR : (p + 1) * PAIR]
    sums = [
        jnp.sum(da.astype(F32), axis=0, keepdims=True),
        jnp.sum(dh2 * normal, axis=0, keepdims=True),
        jnp.sum(dh2, axis=0, keepdims=True),
        jnp.sum(upstream, axis=0, keepdims=True),
    ]
    for half in range(2):
        for n, item in enumerate(sums):
            row = slice(2 + n, 3 + n)
            vec_ref[half, row] = vec_ref[half, row] + item


def middle(mine, x, cot, attn_own, attn_other, vec_in, bfc, weights):
    model = x.shape[1]
    pairs = attn_own.shape[0]
    hidden = bfc.shape[1]
    steps = BIN // BLOCK
    rows = lambda i, m: (i, 0)
    mine_rows = lambda i, m: (m[0] * steps + i, 0)
    return pl.pallas_call(
        middle_kernel,
        out_shape=[
            jax.ShapeDtypeStruct((2, BIN, hidden), BF16),
            jax.ShapeDtypeStruct((2, BIN, hidden), BF16),
            jax.ShapeDtypeStruct((BIN, model), BF16),
            jax.ShapeDtypeStruct((BIN, model), BF16),
            jax.ShapeDtypeStruct((2 * pairs, BIN, PAIR), BF16),
            jax.ShapeDtypeStruct((BIN, model), F32),
            jax.ShapeDtypeStruct((BIN, model), F32),
            jax.ShapeDtypeStruct((2, 16, model), F32),
        ],
        grid_spec=pltpu.PrefetchScalarGridSpec(
            num_scalar_prefetch=1,
            grid=(steps,),
            in_specs=[
                pl.BlockSpec((BLOCK, model), mine_rows),
                pl.BlockSpec((BLOCK, model), mine_rows),
                pl.BlockSpec((pairs, BLOCK, PAIR), lambda i, m: (0, i, 0)),
                pl.BlockSpec((pairs, BLOCK, PAIR), lambda i, m: (0, i, 0)),
                fixed(vec_in.shape), fixed(bfc.shape),
            ]
            + [fixed(w.shape) for w in weights],
            out_specs=[
                pl.BlockSpec((2, BLOCK, hidden), lambda i, m: (0, i, 0)),
                pl.BlockSpec((2, BLOCK, hidden), lambda i, m: (0, i, 0)),
                pl.BlockSpec((BLOCK, model), rows),
                pl.BlockSpec((BLOCK, model), rows),
                pl.BlockSpec((2 * pairs, BLOCK, PAIR), lambda i, m: (0, i, 0)),
                pl.BlockSpec((BLOCK, model), rows),
                pl.BlockSpec((BLOCK, model), rows),
                pl.BlockSpec((2, 16, model), lambda i, m: (0, 0, 0)),
            ],
            scratch_shapes=[pltpu.VMEM(w.shape, BF16) for w in weights[1::2]],
        ),
        compiler_params=pltpu.CompilerParams(vmem_limit_bytes=VMEM_LIMIT),
        cost_estimate=pl.CostEstimate(
            flops=22_000_000_000, bytes_accessed=40_000_000, transcendentals=0
        ),
        name="middle",
    )(mine, x, cot, attn_own, attn_other, vec_in, bfc, *weights)


def proj_grad_kernel(mp_ref, left_ref, right_ref, out_ref):
    out_ref[0] = dot_tn(left_ref[0], right_ref[...])


def proj_grad(mine, g, cot):
    hidden = g.shape[2]
    model = cot.shape[1]
    width = 512
    return pl.pallas_call(
        proj_grad_kernel,
        out_shape=jax.ShapeDtypeStruct((2, hidden, model), F32),
        grid_spec=pltpu.PrefetchScalarGridSpec(
            num_scalar_prefetch=1,
            grid=(2, hidden // width),
            in_specs=[
                pl.BlockSpec((1, BIN, width), lambda h, n, m: (h, 0, n)),
                pl.BlockSpec((BIN, model), lambda h, n, m: (m[0], 0)),
            ],
            out_specs=pl.BlockSpec((1, width, model), lambda h, n, m: (h, n, 0)),
        ),
        compiler_params=pltpu.CompilerParams(vmem_limit_bytes=VMEM_LIMIT),
        name="proj_grad",
    )(mine, g, cot)


def fc_grad_kernel(left_ref, right_ref, out_ref):
    out_ref[0] = dot_tn(left_ref[...], right_ref[0])


def fc_grad(h2, df):
    hidden = df.shape[2]
    model = h2.shape[1]
    return pl.pallas_call(
        fc_grad_kernel,
        out_shape=jax.ShapeDtypeStruct((2, hidden, model), F32),
        grid=(2, hidden // model),
        in_specs=[
            fixed((BIN, model)),
            pl.BlockSpec((1, BIN, model), lambda h, n: (h, 0, n)),
        ],
        out_specs=pl.BlockSpec((1, model, model), lambda h, n: (h, n, 0)),
        compiler_params=pltpu.CompilerParams(vmem_limit_bytes=VMEM_LIMIT),
        name="fc_grad",
    )(h2, df)


def halving_plan(order, rows):
    first, back = [], []
    size = rows
    for n, bit in enumerate(order):
        if n < len(order) - 1 and size % 16 == 0:
            size //= 2
            first.append((bit, size, 0))
            back.append((bit, size, 2))
        else:
            first.append((bit, size, 1))
    return first + back[::-1]


def color_plans(bits):
    orders = [list(range(bits)), list(range(bits))]
    if bits > 1:
        orders[1][:2] = [1, 0]
    return [halving_plan(order, CHUNK // 2) for order in orders]


def attend_back_pair(pair, qkv, dattn, lse_ref, row_ref, dk, dv, vec, pairs):
    dk[...] = jnp.zeros_like(dk)
    dv[...] = jnp.zeros_like(dv)
    half = pair // pairs
    place = pair - half * pairs
    dq_sum = jnp.zeros((1, PAIR), F32)
    for block in range(BIN // BLOCK):
        rows = slice(block * BLOCK, (block + 1) * BLOCK)
        seen = (block + 1) * BLOCK
        queries = qkv[pair, 0, rows]
        upstream = dattn[pair, rows]
        key_rows = qkv[pair, 1, 0:seen]
        value_rows = qkv[pair, 2, 0:seen]
        j = lax.broadcasted_iota(jnp.int32, (seen, BLOCK), 0)
        i = lax.broadcasted_iota(jnp.int32, (seen, BLOCK), 1) + block * BLOCK
        visible = (j >= row_ref[0:1, rows]) & (j <= i)
        dq = jnp.zeros((BLOCK, PAIR), F32)
        for head in range(2):
            masked_q = queries * head_mask(head, score_scale)
            masked_up = upstream * head_mask(head, 1.0)
            scores = dot_nt(key_rows, masked_q)
            probs = jnp.exp(scores - lse_ref[pair, head : head + 1, rows])
            probs = jnp.where(visible, probs, 0.0)
            dprobs = dot_nt(value_rows, masked_up)
            inner = jnp.sum(probs * dprobs, axis=0, keepdims=True)
            dscores = (probs * (dprobs - inner)).astype(BF16)
            dv[0:seen] = dv[0:seen] + dot_nn(probs.astype(BF16), masked_up)
            dk[0:seen] = dk[0:seen] + dot_nn(dscores, masked_q)
            dq = dq + dot_tn(dscores, key_rows * head_mask(head, 1.0))
        dq = (dq * score_scale).astype(BF16)
        qkv[pair, 0, rows] = dq
        dq_sum = dq_sum + jnp.sum(dq.astype(F32), axis=0, keepdims=True)
    dv_low = dv[...].astype(BF16)
    qkv[pair, 1] = dk[...].astype(BF16)
    qkv[pair, 2] = dv_low
    dv_sum = jnp.sum(dv_low.astype(F32), axis=0, keepdims=True)
    width = pairs * PAIR
    vec[half, 8:9, pl.ds(pl.multiple_of(place * PAIR, PAIR), PAIR)] = dq_sum
    vec[half, 8:9, pl.ds(pl.multiple_of(width + place * PAIR, PAIR), PAIR)] = dv_sum


def back_kernel(
    bits, groups,
    gp_ref, gf_ref, qkv_own_ref, qkv_other_ref, dattn_ref, attn_own_ref, attn_other_ref,
    da_ref, h1_ref, w_own_ref, w_other_ref, x_ref, dr1_ref, lse_own_ref, lse_other_ref,
    row_ref, gain_ref, vec_in_ref,
    op_ref, of_ref, oa_ref, ig_ref, vo_ref,
    acc, other, mpbuf, rbufs, qkv, dattn, attn, da, h1, w, x, dh1, ig, lse, dk, dv, vec, vrecv,
    ssem, rsem, mps, mpr, osem, wsem, lsem, igsem, vsem,
):
    dp = lax.axis_index("dp")
    mp = lax.axis_index("mp")
    chunks = 3 * groups
    half_rows = CHUNK // 2
    own_bits = [(dp // (1 << b)) % 2 for b in range(bits)]
    partner = [dp + (1 - 2 * own_bits[b]) * (1 << b) for b in range(bits)]
    plans = color_plans(bits)
    stages = len(plans[0])
    pairs = qkv_own_ref.shape[0]
    model = x_ref.shape[1]
    width = pairs * PAIR

    barrier = pltpu.get_barrier_semaphore()
    for b in range(bits):
        pl.semaphore_signal(barrier, inc=1, device_id=(partner[b], mp), device_id_type=MESH)
    pl.semaphore_signal(barrier, inc=1, device_id=(dp, 1 - mp), device_id_type=MESH)
    pl.semaphore_wait(barrier, bits + 1)

    my_rows = pl.ds(pl.multiple_of(mp * BIN, BIN), BIN)
    loads = []

    def load(src, dst):
        loads.append(pltpu.make_async_copy(src, dst, lsem.at[len(loads)]))

    load(qkv_own_ref, qkv.at[0:pairs])
    load(qkv_other_ref, qkv.at[pairs : 2 * pairs])
    load(dattn_ref, dattn)
    load(lse_own_ref, lse.at[0:pairs])
    load(lse_other_ref, lse.at[pairs : 2 * pairs])
    load(vec_in_ref, vec)
    early = len(loads)
    load(attn_own_ref, attn.at[0:pairs])
    load(attn_other_ref, attn.at[pairs : 2 * pairs])
    load(da_ref, da)
    load(h1_ref, h1)
    load(w_own_ref, w.at[0])
    load(w_other_ref, w.at[1])
    load(x_ref.at[my_rows], x)
    load(dr1_ref, ig)

    starts = []
    for color in range(2):
        base = color * half_rows
        found = []
        for bit, size, kind in plans[color]:
            found.append(base)
            if kind == 0:
                base = base + own_bits[bit] * size
            if kind == 2:
                base = base - own_bits[bit] * size
        starts.append(found)

    def copy(c, color, s):
        bit, size, kind = plans[color][s]
        slot = c % SLOTS
        base = starts[color][s]
        if kind == 0:
            base = base + (1 - own_bits[bit]) * size
        src = acc.at[c, pl.ds(pl.multiple_of(base, 8), size)]
        dst = src if kind == 2 else rbufs[color][s].at[slot]
        return pltpu.make_async_remote_copy(
            src, dst, ssem.at[slot, color, s], rsem.at[slot, color, s],
            device_id=(partner[bit], mp), device_id_type=MESH,
        )

    def finish(c, color, s):
        bit, size, kind = plans[color][s]
        copy(c, color, s).wait()
        base = starts[color][s]
        if kind == 2:
            return
        if kind == 0:
            base = base + own_bits[bit] * size
        rows = pl.ds(pl.multiple_of(base, 8), size)
        acc[c, rows] = acc[c, rows] + rbufs[color][s][c % SLOTS]

    def mp_copy(src, c):
        slot = c % SLOTS
        return pltpu.make_async_remote_copy(
            src, mpbuf.at[slot], mps.at[slot], mpr.at[slot],
            device_id=(dp, 1 - mp), device_id_type=MESH,
        )

    def own_copy(src, c):
        return pltpu.make_async_copy(src, acc.at[c], osem.at[c % SLOTS])

    def chunk_rows(c):
        return pl.ds(pl.multiple_of(c * CHUNK, CHUNK), CHUNK)

    def begin(c):
        @pl.when(c < groups)
        def _():
            mp_copy(gp_ref.at[1, chunk_rows(c)], c).start()
            own_copy(gp_ref.at[0, chunk_rows(c)], c).start()

        @pl.when((c >= groups) & (c < 2 * groups))
        def _():
            mp_copy(gf_ref.at[1, chunk_rows(c - groups)], c).start()
            own_copy(gf_ref.at[0, chunk_rows(c - groups)], c).start()

        @pl.when((c >= 2 * groups) & (c < chunks))
        def _():
            mp_copy(other.at[c - 2 * groups], c).start()

    def out_copy(dst, c):
        return pltpu.make_async_copy(acc.at[c], dst, wsem.at[c % SLOTS])

    def write(c):
        @pl.when(c < groups)
        def _():
            out_copy(op_ref.at[chunk_rows(c)], c).start()

        @pl.when((c >= groups) & (c < 2 * groups))
        def _():
            n = c - groups
            per = model // CHUNK
            cols = pl.ds(pl.multiple_of((n // per) * model, 128), model)
            out_copy(of_ref.at[chunk_rows(n % per), cols], c).start()

        @pl.when(c >= 2 * groups)
        def _():
            out_copy(oa_ref.at[chunk_rows(c - 2 * groups)], c).start()

    def ring_tick(t):
        @pl.when(t < chunks)
        def _():
            mp_copy(other.at[0], t).wait()

            @pl.when(t < 2 * groups)
            def _():
                own_copy(gp_ref.at[0, chunk_rows(0)], t).wait()

            acc[t] = acc[t] + mpbuf[t % SLOTS]

        for s in range(stages):
            c = t - (DELAY + s)

            @pl.when((c >= 0) & (c < chunks))
            def _():
                for color in range(2):
                    finish(c, color, s)

        for s in range(stages)[::-1]:
            c = t - (DELAY + s)

            @pl.when((c >= 0) & (c < chunks))
            def _():
                if s + 1 == stages:
                    write(c)
                else:
                    for color in range(2):
                        copy(c, color, s + 1).start()

        @pl.when(t < chunks)
        def _():
            for color in range(2):
                copy(t, color, 0).start()

        @pl.when(t + AHEAD < chunks)
        def _():
            begin(t + AHEAD)

        c = t - (DELAY + stages)

        @pl.when(c >= 0)
        def _():
            out_copy(op_ref.at[chunk_rows(0)], c).wait()

    def put_grad(half, row, value):
        rows = value.shape[0]
        for piece in range(rows // 128):
            at = row + piece * 128
            block = value[piece * 128 : (piece + 1) * 128]
            dst = (at // CHUNK, slice(at % CHUNK, at % CHUNK + 128))
            if half == 0:
                acc[2 * groups + dst[0], dst[1]] = block
            else:
                other[dst[0], dst[1]] = block

    def side(half, c):
        return jnp.concatenate([qkv[half * pairs + p, c] for p in range(pairs)], axis=1)

    def out_grad(half):
        mixed = jnp.concatenate([attn[half * pairs + p] for p in range(pairs)], axis=1)
        put_grad(half, 0, dot_tn(mixed, da[...]))

    def qkv_grad(half, c):
        low = side(half, c)
        grad = dot_tn(h1[...], low)
        split = model // 2
        put_grad(half, width * (c + 1), jnp.concatenate([grad[:split], grad[split:]], axis=1))
        part = dot_nt(low, w[half, c].astype(BF16))
        if half == 0 and c == 0:
            dh1[...] = part
        else:
            dh1[...] = dh1[...] + part

    def input_grad():
        gain = gain_ref[...].astype(F32)
        gain_sum = jnp.zeros((1, model), F32)
        shift_sum = jnp.zeros((1, model), F32)
        for block in range(BIN // BLOCK):
            rows = slice(block * BLOCK, (block + 1) * BLOCK)
            normal, inverse = norm_parts(x[rows].astype(F32))
            up = dh1[rows]
            gain_sum = gain_sum + jnp.sum(up * normal, axis=0, keepdims=True)
            shift_sum = shift_sum + jnp.sum(up, axis=0, keepdims=True)
            ig[rows] = ig[rows] + norm_back(up, normal, inverse, gain)
        for half in range(2):
            vec[half, 0:1] = gain_sum
            vec[half, 1:2] = shift_sum

    def ig_copies():
        local = pltpu.make_async_copy(ig, ig_ref.at[my_rows], igsem.at[0])
        remote = pltpu.make_async_remote_copy(
            ig, ig_ref.at[my_rows], igsem.at[1], igsem.at[2],
            device_id=(dp, 1 - mp), device_id_type=MESH,
        )
        return local, remote

    def vec_copy(n):
        if n == 0:
            src, device = vec.at[1], (dp, 1 - mp)
        else:
            src, device = vec.at[0], (partner[n - 1], mp)
        return pltpu.make_async_remote_copy(
            src, vrecv.at[n], vsem.at[0, n], vsem.at[1, n], device_id=device, device_id_type=MESH
        )

    for item in loads:
        item.start()
    for c in range(AHEAD):
        begin(c)
    for item in loads[:early]:
        item.wait()

    attend_ticks = 2 * pairs
    grad_tick = attend_ticks
    input_tick = grad_tick + 3
    ticks = chunks + DELAY + stages

    def tick(t, carry):
        ring_tick(t)

        @pl.when(t < attend_ticks)
        def _():
            attend_back_pair(t, qkv, dattn, lse, row_ref, dk, dv, vec, pairs)

        for c in range(3):
            @pl.when(t == grad_tick + c)
            def _():
                if c == 0:
                    for item in loads[early:]:
                        item.wait()
                    out_grad(0)
                    out_grad(1)
                qkv_grad(0, c)
                qkv_grad(1, c)

        @pl.when(t == input_tick)
        def _():
            input_grad()
            for item in ig_copies():
                item.start()
            vec_copy(0).start()

        for n in range(bits + 1):
            @pl.when(t == input_tick + 1 + n)
            def _():
                vec_copy(n).wait()
                vec[0] = vec[0] + vrecv[n]
                if n < bits:
                    vec_copy(n + 1).start()

        return carry

    lax.fori_loop(0, ticks, tick, 0)
    for item in ig_copies():
        item.wait()
    vo_ref[...] = vec[0]


def back(bits, proj, fc, arrays, row, gain, vec, sizes):
    pairs, hidden, model = sizes
    width = pairs * PAIR
    groups = hidden // CHUNK
    chunks = 3 * groups
    plans = color_plans(bits)
    stages = len(plans[0])
    recv = [
        [pltpu.VMEM((SLOTS, size, model), F32) for _, size, kind in plan if kind < 2]
        for plan in plans
    ]
    here = pl.BlockSpec(memory_space=pl.ANY)
    vmem = pl.BlockSpec(memory_space=pltpu.VMEM)
    dma = pltpu.SemaphoreType.DMA
    return pl.pallas_call(
        functools.partial(back_kernel, bits, groups),
        out_shape=[
            jax.ShapeDtypeStruct((hidden, model), F32),
            jax.ShapeDtypeStruct((model, hidden), F32),
            jax.ShapeDtypeStruct((4 * width, model), F32),
            jax.ShapeDtypeStruct((2 * BIN, model), F32),
            jax.ShapeDtypeStruct((16, model), F32),
        ],
        in_specs=[here] * (2 + len(arrays)) + [vmem, vmem, here],
        out_specs=[here] * 4 + [vmem],
        scratch_shapes=[
            pltpu.VMEM((chunks, CHUNK, model), F32),
            pltpu.VMEM((groups, CHUNK, model), F32),
            pltpu.VMEM((SLOTS, CHUNK, model), F32),
            recv,
            pltpu.VMEM((2 * pairs, 3, BIN, PAIR), BF16),
            pltpu.VMEM((2 * pairs, BIN, PAIR), BF16),
            pltpu.VMEM((2 * pairs, BIN, PAIR), BF16),
            pltpu.VMEM((BIN, model), BF16),
            pltpu.VMEM((BIN, model), BF16),
            pltpu.VMEM((2, 3, model, width), F32),
            pltpu.VMEM((BIN, model), BF16),
            pltpu.VMEM((BIN, model), F32),
            pltpu.VMEM((BIN, model), F32),
            pltpu.VMEM((2 * pairs, 8, BIN), F32),
            pltpu.VMEM((BIN, PAIR), F32),
            pltpu.VMEM((BIN, PAIR), F32),
            pltpu.VMEM((2, 16, model), F32),
            pltpu.VMEM((bits + 1, 16, model), F32),
            dma((SLOTS, 2, stages)),
            dma((SLOTS, 2, stages)),
            dma((SLOTS,)),
            dma((SLOTS,)),
            dma((SLOTS,)),
            dma((SLOTS,)),
            dma((14,)),
            dma((3,)),
            dma((2, bits + 1)),
        ],
        compiler_params=pltpu.CompilerParams(
            collective_id=0, has_side_effects=True, vmem_limit_bytes=67_000_000
        ),
        name="back",
    )(proj, fc, *arrays, row, gain, vec)


def on_device(
    tokens, segments, lengths, ln1_gain, ln1_bias, w_qkv, b_qv, w_out, out_bias,
    ln2_gain, ln2_bias, w_fc, b_fc, w_proj, proj_bias, cotangent,
):
    model = tokens.shape[1]
    width = w_qkv.shape[2]
    hidden = w_fc.shape[1]
    pairs = width // PAIR
    groups = lax.axis_size("dp")
    bits = groups.bit_length() - 1
    if lax.axis_size("mp") != 2 or groups != 1 << bits or tokens.shape[0] != 2 * BIN:
        raise ValueError("unsupported mesh")
    side = lax.axis_index("mp")
    mine = side.astype(jnp.int32).reshape(1)
    swap = [(0, 1), (1, 0)]

    def cross(value):
        return lax.ppermute(value, "mp", swap)

    w3 = jnp.transpose(w_qkv, (1, 0, 2)).astype(F32)
    small = jnp.concatenate([b_qv.reshape(-1), b_fc]).astype(F32)
    small_other = cross(small)
    w3_other = cross(w3)
    wo_other = cross(w_out.astype(F32))
    wf_other = cross(w_fc.astype(F32))
    wp_other = cross(w_proj.astype(F32))

    def qkv_bias(flat):
        return jnp.stack([flat[:width], jnp.zeros((width,), F32), flat[width : 2 * width]])

    own, other_front = front(
        mine, tokens, segments.reshape(2, BIN), lengths,
        ln1_gain.reshape(1, -1), ln1_bias.reshape(1, -1), w3, qkv_bias(small), width,
    )
    qkv_own, attn_own, lse_own, h1, start, row = own
    qkv_other, attn_other, lse_other = other_front(h1, start, w3_other, qkv_bias(small_other))
    vec_in = jnp.stack([out_bias, ln2_gain, ln2_bias, proj_bias]).astype(F32)
    bfc = jnp.stack([small[2 * width :], small_other[2 * width :]])
    g, df, h2, da, dattn, dr1, block_sum, vec = middle(
        mine, tokens, cotangent, attn_own, attn_other, vec_in, bfc,
        (w_out, wo_other, w_fc, wf_other, w_proj, wp_other),
    )
    sum_other = cross(block_sum)
    proj = proj_grad(mine, g, cotangent)
    fc = fc_grad(h2, df)
    arrays = (
        qkv_own, qkv_other, dattn, attn_own, attn_other, da, h1, w3, w3_other, tokens, dr1,
        lse_own, lse_other,
    )
    grad_proj, grad_fc, grad_attn, input_grad, rows = back(
        bits, proj, fc, arrays, row, ln1_gain.reshape(1, -1), vec, (pairs, hidden, model)
    )
    first = jnp.where(side == 0, block_sum, sum_other)
    second = jnp.where(side == 0, sum_other, block_sum)
    block_out = (jnp.concatenate([first, second]) + vec_in[3]).astype(BF16)
    grad_out = grad_attn[:width]
    grad_qkv = grad_attn[width:].reshape(3, width, 2, width)
    grad_qkv = jnp.transpose(grad_qkv, (2, 1, 0, 3)).reshape(model, 3, width)
    return (
        block_out,
        input_grad,
        rows[0],
        rows[1],
        grad_qkv,
        rows[8].reshape(2, width),
        grad_out,
        rows[2],
        rows[3],
        rows[4],
        grad_fc,
        rows[6:8].reshape(-1),
        grad_proj,
        rows[5],
    )


def solution(mesh):
    rows = P("dp", None)
    placed = (
        rows, P("dp"), rows, P(), P(), P(None, None, "mp"), P(None, "mp"), P("mp", None), P(),
        P(), P(), P(None, "mp"), P("mp"), P("mp", None), P(), rows,
    )
    results = (
        rows, rows, P(), P(), P(None, None, "mp"), P(None, "mp"), P("mp", None), P(), P(), P(),
        P(None, "mp"), P("mp"), P("mp", None), P(),
    )
    return jax.shard_map(
        on_device, mesh=mesh, in_specs=placed, out_specs=results, check_vma=False
    )
```

time: 1440 us -> 428 us (0.30)
  waiting for transfers between devices: 823 us -> 10.8 us
  Pallas kernels: 0 us -> 363 us
  matrix products: 246 us -> 0 us
  local copies, waits for them, and re-layouts: 221 us -> 28.5 us
  other arithmetic: 113 us -> 15.9 us
  between operations: 16.1 us -> 1.14 us
    unnamed x7 -> x0, waiting for transfers between devices: 772 us -> none
    pallas_call x0 -> x6, Pallas kernels: none -> 363 us  [the longest x1 262 us: back(): pl.pallas_call(functools.partial(back_kernel, bits, groups), out_shape=[j...]
    dot_general x26 -> x0, matrix products: 246 us -> none  [the longest x4 41.4 us: masked_scores(): jnp.einsum('qhd,khd->hqk', queries, key_rows, preferred_element_type=jnp....]
    unnamed x104 -> x43, local copies, waits for them, and re-layouts: 91.7 us -> 10.3 us
    reduce_sum x11 -> x0, other arithmetic: 54.5 us -> none  [the longest x2 22.4 us: attend_forward(): totals = jnp.sum(weights, axis=-1, keepdims=True)]
    psum x3 -> x0, waiting for transfers between devices: 50.6 us -> none  [the longest x1 34.9 us: on_device(): first_sum = inputs_f + lax.psum(attn_part, 'mp') + out_shift]
    reshape x10 -> x6, local copies, waits for them, and re-layouts: 44.7 us -> 5.7 us  [the longest x1 3.31 us: on_device(): grad_qkv = grad_attn[width:].reshape(3, width, 2, width)]
    while x12 -> x0, local copies, waits for them, and re-layouts: 30.8 us -> none  [the longest x2 12.4 us: on_device(): lax.map(attend_backward, (joined_bins, seg_bins, start_bins, log_totals,...]
  transfers between devices with their start and end apart: 5 -> 6, of which waited for: 4 -> 1; matrix products, arithmetic and copies ran while one was open for 7% -> 6% of each run, Pallas kernels for 0% -> 76%
where the time goes in v1:
time: 428 us; the launch traced here: 422 us
  Pallas kernels  363 us (85%)
  local copies, waits for them, and re-layouts  28.5 us (7%)
  other arithmetic  15.9 us (4%)
  waiting for transfers between devices  10.8 us (3%)
    pallas_call x1, Pallas kernels, back(): pl.pallas_call(functools.partial(back_kernel, bits, groups), out_shape=[j...  262 us
    pallas_call x1, Pallas kernels, middle(): pl.pallas_call(middle_kernel, out_shape=[jax.ShapeDtypeStruct((2, BIN, hi...  40.9 us
    pallas_call x1, Pallas kernels, front(): return (own(mine, x, seg, lens, gain, shift, w_own, bias_own), other)  20.4 us
    pallas_call x1, Pallas kernels, other(): pl.pallas_call(other_front_kernel, out_shape=out_shapes, grid=(pairs,), i...  18.8 us
    pallas_call x1, Pallas kernels, proj_grad(): pl.pallas_call(proj_grad_kernel, out_shape=jax.ShapeDtypeStruct((2, hidde...  10.9 us
    ppermute x6, waiting for transfers between devices, cross(): return lax.ppermute(value, 'mp', swap)  10.8 us
    unnamed x43, local copies, waits for them, and re-layouts  10.3 us
    pallas_call x1, Pallas kernels, fc_grad(): pl.pallas_call(fc_grad_kernel, out_shape=jax.ShapeDtypeStruct((2, hidden,...  10 us
  transfers between devices with their start and end apart: 6, of which 1 were waited for; matrix products, arithmetic and copies ran while one was open for 6% of the time, Pallas kernels for 76%

profile of v1, /device:TPU:0, one launch (start us, length us, event | category | flops | bytes accessed | tf_op | source)
XLA Modules:
  0.0 421.8 jit_solution(9571428499698374914)
XLA Ops:
  0.6 0.0 copy-start.1
  0.7 4.4 %convert_element_type.29 = f32[1536,768]{1,0:T(8,128)} convert(bf16[1536,768]{1,0:T(8,128)(2,1)} %wp_own_ref.1) | non-fusion elementwise | flops 1179648 | bytes 7077888 | tf_op jit(solution)/shard_map/convert_element_type | solution.py:807
  5.0 0.5 collective-permute-start.4
  5.5 2.8 convert_element_type.28
  8.4 0.0 copy-start.7
  8.4 0.0 copy-start.8
  8.4 0.0 copy-start.9
  8.4 0.0 copy-start.10
  8.4 0.0 copy-start.11
  8.4 0.0 copy-start.4
  8.4 0.1 collective-permute-start.3
  8.5 2.0 convert_bitcast_fusion.w_ref.w_own_ref
  10.5 0.5 collective-permute-start
  11.1 0.1 collective-permute-start.1
  11.2 0.1 convert_element_type.27
  11.2 0.5 collective-permute-start.2
  11.9 0.6 maximum_convert_fusion.1.vec_in_ref
  12.5 0.6 reshape.55.gain_ref
  13.1 0.6 reshape.56.shift_ref
  13.7 0.6 reshape.54.seg_ref
  14.3 0.1 pad.12.clone
  14.4 10.8 %collective-permute-done.1 = f32[2304]{0:T(1024)S(1)} collective-permute-done((f32[2304]{0:T(1024)S(1)}, f32[2304]{0:T(1024)S(1)}, u32[]{:S(2)}, u32[]{:S(2)}) %collective-permute-start.1) | collective-permute-done | bytes 9248 | tf_op jit(solution)/shard_map/ppermute | solution.py:799
  25.2 0.6 pad_maximum_fusion.bfc_ref
  25.9 0.7 pad_maximum_fusion.2
  26.5 20.4 %own_front.1 = (bf16[3,3,1024,128]{3,2,1,0:T(8,128)(2,1)}, bf16[3,1024,128]{2,1,0:T(8,128)(2,1)}, f32[3,8,1024]{2,1,0:T(8,128)}, bf16[1024,768]{1,0:T(8,128)(2,1...) custom-call(s32[1]{0:T(128)} %bitcast.mp_ref, bf16[2048,768]{1,0:T(8,128)(2,1)} %x_ref.5, s32[2,1024]{1,0:T(2,128)} %reshape.54.seg_ref, ...), custom_call_target="tpu_custom_call" | custom-call | flops 6000000000 | bytes 10000000 | tf_op jit(solution)/shard_map/own_front/pallas_call | solution.py:201
  46.9 18.8 %other_front.1 = (bf16[3,3,1024,128]{3,2,1,0:T(8,128)(2,1)}, bf16[3,1024,128]{2,1,0:T(8,128)(2,1)}, f32[3,8,1024]{2,1,0:T(8,128)}) custom-call(bf16[1024,768]{1,0:T(8,128)(2,1)} %get-tuple-element.37.h1_ref, s32[1024,1]{1,0:T(8,128)} %get-tuple-element.38.start_ref, f32[3,768,384]{2,1,0:T(8,128)} %collective-permute-done.w_ref.w_other_ref, ...), custom_call_target="tpu_custom_call" | custom-call | flops 6000000000 | bytes 10000000 | tf_op jit(solution)/shard_map/other_front/pallas_call | solution.py:190
  65.7 1.0 copy-done.13
  66.7 40.9 %middle.1 = (bf16[2,1024,1536]{2,1,0:T(8,128)(2,1)}, bf16[2,1024,1536]{2,1,0:T(8,128)(2,1)}, bf16[1024,768]{1,0:T(8,128)(2,1)}, bf16[1024,768]{1,0:T(8,128)(2,1)...) custom-call(s32[1]{0:T(128)} %bitcast.mp_ref, ...), custom_call_target="tpu_custom_call" | custom-call | flops 22000001024 | bytes 40000000 | tf_op jit(solution)/shard_map/middle/pallas_call | solution.py:280
  107.7 0.4 collective-permute-start.5
  108.1 0.7 slice_reduce_fusion
  108.8 10.9 %proj_grad.1.gp_ref = f32[2,1536,768]{2,1,0:T(8,128)} custom-call(s32[1]{0:T(128)} %bitcast.mp_ref, bf16[2,1024,1536]{2,1,0:T(8,128)(2,1)} %get-tuple-element.41.left_ref, bf16[2048,768]{1,0:T(8,128)(2,1)} %right_ref.1), custom_call_target="tpu_custom_call" | custom-call | tf_op jit(solution)/shard_map/proj_grad/pallas_call | solution.py:331
  119.7 10.0 %fc_grad.1.gf_ref = f32[2,1536,768]{2,1,0:T(8,128)} custom-call(bf16[1024,768]{1,0:T(8,128)(2,1)} %get-tuple-element.42.left_ref, bf16[2,1024,1536]{2,1,0:T(8,128)(2,1)} %get-tuple-element.43.right_ref), custom_call_target="tpu_custom_call" | custom-call | tf_op jit(solution)/shard_map/fc_grad/pallas_call | solution.py:355
  129.8 262.3 %back.1 = (f32[1536,768]{1,0:T(8,128)}, f32[768,1536]{1,0:T(8,128)}, f32[1536,768]{1,0:T(8,128)}, f32[2048,768]{1,0:T(8,128)}, f32[16,768]{1,0:T(8,128)}) custom-call(f32[2,1536,768]{2,1,0:T(8,128)} %proj_grad.1.gp_ref, f32[2,1536,768]{2,1,0:T(8,128)} %fc_grad.1.gf_ref, bf16[3,3,1024,128]{3,2,1,0:T(8,128)(2,1)} %get-tuple-element.44.qkv_own_ref, ...), custom_call_target="tpu_custom_call" | custom-call | tf_op jit(solution)/shard_map/back/pallas_call | solution.py:735
  392.0 2.4 slice.62
  394.4 2.2 slice.60
  396.6 0.7 slice.66
  397.4 0.6 reshape.60
  398.0 1.6 slice_reduce_fusion.1
  399.6 0.6 reshape_squeeze.3
  400.2 3.3 reshape.58
  403.5 4.2 copy.30
  407.7 2.5 broadcast_select_fusion.1
  410.2 2.2 fusion
  412.4 3.2 copy.34
  415.6 0.3 slice-done.5
  415.9 2.4 copy.35
  418.3 1.1 slice-done.3
  419.4 2.2 copy.36
  (54 shorter events, 0.2 us)
Async XLA Ops:
  0.6 4.9 %copy-start.1 = (bf16[768,1536]{1,0:T(8,128)(2,1)S(1)}, bf16[768,1536]{1,0:T(8,128)(2,1)}, u32[]{:S(2)}) copy-start(bf16[768,1536]{1,0:T(8,128)(2,1)} %wf_own_ref.1) | copy-start | bytes 7077892
  5.0 3.5 copy-start.2
  5.0 60.7 %collective-permute-start.4 = (f32[1536,768]{1,0:T(8,128)}, f32[1536,768]{1,0:T(8,128)}, u32[]{:S(2)}, u32[]{:S(2)}) collective-permute-start(f32[1536,768]{1,0:T(8,128)} %convert_element_type.29), channel_id=1, source_target_pairs={{0,1},{1,0},{2,3},{3,2},{4,5},{5,4},{6,7},{7,6},{8,9},{9,8},{10,11... | collective-permute-start | bytes 14155784 | tf_op jit(solution)/shard_map/ppermute | solution.py:799
  8.3 2.7 copy-start.12
  8.3 2.7 copy-start.5
  8.3 2.8 copy-start.3
  8.3 3.4 copy-start.6
  8.4 3.4 copy-start.7
  8.4 3.5 copy-start.8
  8.4 3.5 copy-start.9
  8.4 4.1 copy-start.10
  8.4 4.7 %copy-start.11 = (bf16[768]{0:T(1024)(128)(2,1)S(1)}, bf16[768]{0:T(1024)(128)(2,1)}, u32[]{:S(2)}) copy-start(bf16[768]{0:T(1024)(128)(2,1)} %param.20) | copy-start | bytes 4612
  8.4 5.3 %copy-start.4 = (s32[2048]{0:T(1024)S(1)}, s32[2048]{0:T(1024)}, u32[]{:S(2)}) copy-start(s32[2048]{0:T(1024)} %param.17) | copy-start | bytes 24580
  8.4 57.3 %collective-permute-start.3 = (f32[768,1536]{1,0:T(8,128)}, f32[768,1536]{1,0:T(8,128)}, u32[]{:S(2)}, u32[]{:S(2)}) collective-permute-start(f32[768,1536]{1,0:T(8,128)} %convert_element_type.28), channel_id=1, source_target_pairs={{0,1},{1,0},{2,3},{3,2},{4,5},{5,4},{6,7},{7,6},{8,9},{9,8},{10,11... | collective-permute-start | bytes 14155784 | tf_op jit(solution)/shard_map/ppermute | solution.py:799
  10.5 36.4 %collective-permute-start = (f32[3,768,384]{2,1,0:T(8,128)}, f32[3,768,384]{2,1,0:T(8,128)}, u32[]{:S(2)}, u32[]{:S(2)}) collective-permute-start(f32[3,768,384]{2,1,0:T(8,128)} %convert_bitcast_fusion.w_ref.w_own_ref), channel_id=1, source_target_pairs={{0,1},{1,0},{2,3},{3,2},{4,5},{5,4},{6,7},{7,6},{8,9},{9,8},{10,11... | collective-permute-start | bytes 10616840 | tf_op jit(solution)/shard_map/ppermute | solution.py:799
  11.1 14.1 %collective-permute-start.1 = (f32[2304]{0:T(1024)S(1)}, f32[2304]{0:T(1024)S(1)}, u32[]{:S(2)}, u32[]{:S(2)}) collective-permute-start(f32[2304]{0:T(1024)S(1)} %maximum_convert_fusion), channel_id=1, source_target_pairs={{0,1},{1,0},{2,3},{3,2},{4,5},{5,4},{6,7},{7,6},{8,9},{9,8},{10,11... | collective-permute-start | bytes 27656 | tf_op jit(solution)/shard_map/ppermute | solution.py:799
  11.2 54.5 %collective-permute-start.2 = (f32[384,768]{1,0:T(8,128)S(1)}, f32[384,768]{1,0:T(8,128)S(1)}, u32[]{:S(2)}, u32[]{:S(2)}) collective-permute-start(f32[384,768]{1,0:T(8,128)S(1)} %convert_element_type.27), channel_id=1, source_target_pairs={{0,1},{1,0},{2,3},{3,2},{4,5},{5,4},{6,7},{7,6},{8,9},{9,8},{10,11... | collective-permute-start | bytes 3538952 | tf_op jit(solution)/shard_map/ppermute | solution.py:799
  65.7 1.0 copy-start.13
  107.7 300.0 %collective-permute-start.5 = (f32[1024,768]{1,0:T(8,128)}, f32[1024,768]{1,0:T(8,128)}, u32[]{:S(2)}, u32[]{:S(2)}) collective-permute-start(f32[1024,768]{1,0:T(8,128)} %get-tuple-element.40), channel_id=1, source_target_pairs={{0,1},{1,0},{2,3},{3,2},{4,5},{5,4},{6,7},{7,6},{8,9},{9,8},{10,11... | collective-permute-start | bytes 9437192 | tf_op jit(solution)/shard_map/ppermute | solution.py:799
  403.5 4.2 copy-start
  407.7 4.7 %slice-start = ((s8[6291456]{0:T(1024)(128)(4,1)}), s8[4194304]{0:T(1024)(128)(4,1)S(1)}, s32[]{:S(2)}) async-start(s8[6291456]{0:T(1024)(128)(4,1)} %bitcast.7), calls=%async_computation | async-start | bytes 8388608
  407.7 4.7 %slice-start.1 = ((s8[6291456]{0:T(1024)(128)(4,1)}), s8[2097152]{0:T(1024)(128)(4,1)S(1)}, s32[]{:S(2)}) async-start(s8[6291456]{0:T(1024)(128)(4,1)} %bitcast.7), calls=%async_computation.1 | async-start | bytes 4194304
  410.2 5.4 %slice-start.4 = ((s8[4718592]{0:T(1024)(128)(4,1)}), s8[4194304]{0:T(1024)(128)(4,1)S(1)}, s32[]{:S(2)}) async-start(s8[4718592]{0:T(1024)(128)(4,1)} %bitcast.11), calls=%async_computation.4 | async-start | bytes 8388608
  410.2 8.1 %slice-start.2 = ((s8[4718592]{0:T(1024)(128)(4,1)}), s8[524288]{0:T(1024)(128)(4,1)S(1)}, s32[]{:S(2)}) async-start(s8[4718592]{0:T(1024)(128)(4,1)} %bitcast.9), calls=%async_computation.2 | async-start | bytes 1048576
  412.4 3.5 slice-start.5
  412.4 7.0 %slice-start.3 = ((s8[4718592]{0:T(1024)(128)(4,1)}), s8[4194304]{0:T(1024)(128)(4,1)S(1)}, s32[]{:S(2)}) async-start(s8[4718592]{0:T(1024)(128)(4,1)} %bitcast.9), calls=%async_computation.3 | async-start | bytes 8388608
